TPU v7x, 32 devices: a whole 2x2x4 slice. The times are simulated.
32 devices in a mesh: row: 4 (over y, x), col: 8 (over z, core).
Axes of the slice: x: 2, y: 2, z: 4, core: 2. Of those that a mesh axis runs over, the one named last changes fastest.
Arguments:
- object_tiles: float32 [2, 2, 1024, 2048], P(None, None, 'row', 'col'), may hold values from -5 to 5
- probe_modes: float32 [2, 4, 128, 128], replicated, may hold values from -6 to 6
- offsets: int32 [4, 8, 3, 2], P('row', 'col'), may hold values from 0 to 192
- amplitude: float32 [4, 8, 3, 128, 128], P('row', 'col'), may hold values from 0.2 to 3
Outputs:
- object_grad: float32 [2, 2, 1024, 2048], P(None, None, 'row', 'col')
- probe_new: float32 [2, 4, 128, 128], replicated
All inputs are finite; a program needn't handle non-finite values.
Results may differ from a plain program's by a relative error of at most 0.0003.
Values sent between devices are 32-bit elements; how exact they have to be, the bound alone decides.
A program may use at most 64 MiB of HBM per device.

v0:
```python
import functools

import jax
import jax.numpy as jnp
import numpy as np
from jax import lax
from jax.experimental import pallas as pl
from jax.experimental.pallas import tpu as pltpu
from jax.sharding import PartitionSpec as P

HALO = 32
PROP = 0.002
SHIFT_AMP = 0.5
STEP_SIZE = 0.5
EPSILON = 1e-06
LANES = 128
SUB = 8
MESH = pl.DeviceIdType.MESH
F32 = jnp.float32
BF16 = jnp.bfloat16


def tables(win):
    k = np.arange(win)
    c = np.exp(-2j * np.pi * (k[:, None] * k[None, :] % win) / win) / np.sqrt(win)
    freq = (k + win // 2) % win - win // 2
    kern = np.conj(c) @ np.diag(np.exp(-1j * PROP * freq**2)) @ c
    out = []
    for m in (c, np.conj(c), kern, np.conj(kern)):
        full = np.block([[m.real, m.imag], [-m.imag, m.real]])
        high = full.astype(np.float32).astype(jnp.bfloat16)
        low = (full - high.astype(np.float64)).astype(np.float32).astype(jnp.bfloat16)
        out += [high, low]
    return np.stack(out)


FWD, INV, KER, KER_INV = 0, 1, 2, 3


def split(x):
    high = x.astype(BF16)
    return high, (x - high.astype(F32)).astype(BF16)


def dot(a, b):
    return jnp.dot(a, b, preferred_element_type=F32)


def right(x, tab, which):
    high, low = split(x)
    return dot(high, tab[2 * which]) + (
        dot(low, tab[2 * which]) + dot(high, tab[2 * which + 1])
    )


def left(x, tab, which):
    high, low = split(x)
    which = which ^ 1
    return dot(tab[2 * which], high) + (
        dot(tab[2 * which], low) + dot(tab[2 * which + 1], high)
    )


def swap(y):
    w = y.shape[0] // 2
    top = jnp.concatenate([y[:w, :w], y[w:, :w]], axis=1)
    low = jnp.concatenate([y[:w, w:], y[w:, w:]], axis=1)
    return jnp.concatenate([top, low], axis=0)


def twice(x, axis):
    return jnp.concatenate([x, x], axis=axis)


def lane(rows):
    return lax.broadcasted_iota(jnp.int32, (rows, LANES), 1)


CHANS = [(part, lay) for part in range(2) for lay in range(2)]
EVERY = slice(None)


def packed(get, first, rows, count=4):
    out = None
    for ch in range(count):
        shift = (HALO * ch - first) % LANES
        block = get(ch)
        block = pltpu.roll(block, shift, 1) if shift else block
        at = lane(rows)
        keep = (at >= HALO * ch) & (at < HALO * ch + HALO)
        out = jnp.where(keep, block, 0.0 if out is None else out)
    return out


def unpacked(block, ch, first):
    shift = (first - HALO * ch) % LANES
    return pltpu.roll(block, shift, 1) if shift else block


def send(src, dst, ssem, rsem, i, to):
    copy = pltpu.make_async_remote_copy(
        src_ref=src,
        dst_ref=dst,
        send_sem=ssem.at[i],
        recv_sem=rsem.at[i],
        device_id=to,
        device_id_type=MESH,
    )
    copy.start()
    return copy


def places(n_row, n_col):
    my_r = lax.axis_index("row")
    my_c = lax.axis_index("col")
    up = lax.rem(my_r + n_row - 1, n_row)
    down = lax.rem(my_r + 1, n_row)
    lft = lax.rem(my_c + n_col - 1, n_col)
    rgt = lax.rem(my_c + 1, n_col)
    return my_r, my_c, up, down, lft, rgt


def zones(tile):
    head, tail = pl.ds(0, HALO), pl.ds(tile - HALO, HALO)
    mid, after, body = pl.ds(HALO, tile), pl.ds(HALO + tile, HALO), pl.ds(0, tile)
    return head, tail, mid, after, body


def rows_of(p, win):
    return [[(4 * p + 2 * part + m) * win for m in range(2)] for part in range(2)]


def halo_kernel(
    sizes, obj_ref, ext, pack_l, pack_r, halo_l, halo_r, h_send, h_recv
):
    n_row, n_col = sizes
    tile = obj_ref.shape[2]
    tall = tile + 2 * HALO
    wide = tile + LANES
    my_r, my_c, up, down, lft, rgt = places(n_row, n_col)
    head, tail, mid, after, body = zones(tile)
    barrier = pltpu.get_barrier_semaphore()
    around = [(r, c) for r in (up, my_r, down) for c in (lft, my_c, rgt)]
    del around[4]
    for to in around:
        pl.semaphore_signal(barrier, inc=1, device_id=to, device_id_type=MESH)
    pack_l[...] = packed(lambda ch: obj_ref[CHANS[ch] + (EVERY, slice(0, LANES))], 0, tile)
    pack_r[...] = packed(
        lambda ch: obj_ref[CHANS[ch] + (EVERY, slice(tile - LANES, tile))], LANES - HALO, tile
    )
    pl.semaphore_wait(barrier, 8)
    halo = [
        send(obj_ref.at[:, :, tail, :], ext.at[:, :, head, body], h_send, h_recv, 0, (down, my_c)),
        send(obj_ref.at[:, :, head, :], ext.at[:, :, after, body], h_send, h_recv, 1, (up, my_c)),
        send(pack_r, halo_l.at[mid], h_send, h_recv, 2, (my_r, rgt)),
        send(pack_l, halo_r.at[mid], h_send, h_recv, 3, (my_r, lft)),
        send(pack_r.at[tail], halo_l.at[head], h_send, h_recv, 4, (down, rgt)),
        send(pack_r.at[head], halo_l.at[after], h_send, h_recv, 5, (up, rgt)),
        send(pack_l.at[tail], halo_r.at[head], h_send, h_recv, 6, (down, lft)),
        send(pack_l.at[head], halo_r.at[after], h_send, h_recv, 7, (up, lft)),
    ]
    ext[:, :, mid, body] = obj_ref[...]
    ext[:, :, pl.ds(tall, SUB), :] = jnp.zeros((2, 2, SUB, wide), F32)
    for copy in halo:
        copy.wait()
    for ch in range(4):
        near = unpacked(halo_r[...], ch, 0)
        far_side = unpacked(halo_l[...], ch, LANES - HALO)
        at = lane(tall)
        edge = jnp.where(at < HALO, near, jnp.where(at >= LANES - HALO, far_side, 0.0))
        ext[CHANS[ch] + (pl.ds(0, tall), pl.ds(tile, LANES))] = edge


def window_kernel(sizes, off_ref, ext, winds):
    win, scans = sizes
    wide = ext.shape[3]

    @pl.loop(0, scans)
    def _(s):
        row = off_ref[0, 0, 0, s]
        base = pl.multiple_of(row - lax.rem(row, SUB), SUB)
        rest = lax.rem(win + SUB - lax.rem(row, SUB), win + SUB)
        shift = lax.rem(wide + HALO - off_ref[0, 0, 1, s], wide)
        for ch, (part, lay) in enumerate(CHANS):
            block = ext[part, lay, pl.ds(base, win + SUB), :]
            block = pltpu.roll(block, shift, 1)[:, :win]
            winds[s, ch] = pltpu.roll(block, rest, 0)[:win]


def main_kernel(
    sizes,
    off_ref,
    winds,
    probe_ref,
    amp_ref,
    tab,
    grad_ref,
    new_ref,
    wave,
    far,
    factor,
    gobj,
    gprobe,
    acc,
    total,
    spread,
    from_top,
    from_bot,
    edge_l,
    edge_r,
    from_l,
    from_r,
    half_in,
    half_sum,
    parts,
    g_send,
    g_recv,
    pair_send,
    pair_recv,
    rs_send,
    rs_recv,
    ag_send,
    ag_recv,
    fw_send,
    fw_recv,
):
    n_row, n_col, win, scans, chunks = sizes
    n_dev = n_row * n_col
    n_half = n_col // 2
    group = n_row * n_half
    tile = grad_ref.shape[2]
    tall, wide = tile + 2 * HALO, tile + LANES
    my_r, my_c, up, down, lft, rgt = places(n_row, n_col)
    head, tail, mid, after, body = zones(tile)
    me = my_r * n_col + my_c
    barrier = pltpu.get_barrier_semaphore()

    @pl.loop(1, n_dev)
    def _(k):
        other = lax.rem(me + k, n_dev)
        where = (other // n_col, lax.rem(other, n_col))
        pl.semaphore_signal(barrier, inc=1, device_id=where, device_id_type=MESH)

    gprobe[...] = jnp.zeros_like(gprobe)
    gobj[...] = jnp.zeros_like(gobj)

    @pl.loop(0, scans)
    def _(s):
        o = {chan: winds[s, ch] for ch, chan in enumerate(CHANS)}
        power = None
        for p in range(2):
            rows = []
            for m in range(2):
                pr, pi = probe_ref[0, 2 * p + m], probe_ref[1, 2 * p + m]
                rows.append(
                    jnp.concatenate(
                        [
                            pr * o[0, 0] - pi * o[1, 0],
                            pr * o[1, 0] + pi * o[0, 0],
                        ],
                        axis=1,
                    )
                )
            psi = jnp.concatenate(rows, axis=0)
            w = left(swap(right(psi, tab, KER)), tab, KER)
            wave[s, p] = w
            wr, wi = w[:win], w[win:]
            o1r, o1i = twice(o[0, 1], 1), twice(o[1, 1], 1)
            psi = jnp.concatenate([wr * o1r - wi * o1i, wr * o1i + wi * o1r], axis=0)
            psi = right(swap(left(psi, tab, FWD)), tab, FWD)
            far[s, p] = psi
            sq = psi * psi
            part_sum = (sq[:win, :win] + sq[:win, win:]) + (sq[win:, :win] + sq[win:, win:])
            power = part_sum if power is None else power + part_sum
        root = jnp.sqrt(power + SHIFT_AMP)
        factor[s] = 2.0 * (root - amp_ref[0, 0, s]) / root


    def first_half(p, s):
        g = far[s, p] * twice(twice(factor[s], 0), 1)
        g = left(swap(right(g, tab, INV)), tab, INV)
        w = wave[s, p]
        gr, gi, wr, wi = g[:win], g[win:], w[:win], w[win:]
        re = wr * gr + wi * gi
        im = wr * gi - wi * gr
        gobj[1, 0, s] += re[:, :win] + re[:, win:]
        gobj[1, 1, s] += im[:, :win] + im[:, win:]
        o1r, o1i = twice(winds[s, 1], 1), twice(winds[s, 3], 1)
        far[s, p] = jnp.concatenate([o1r * gr + o1i * gi, o1r * gi - o1i * gr], axis=0)

    def second_half(p, s):
        g = right(swap(left(far[s, p], tab, KER_INV)), tab, KER_INV)
        o0r, o0i = winds[s, 0], winds[s, 2]
        re = im = None
        for m in range(2):
            gr, gi = g[m * win : (m + 1) * win, :win], g[m * win : (m + 1) * win, win:]
            pr, pi = probe_ref[0, 2 * p + m], probe_ref[1, 2 * p + m]
            a = pr * gr + pi * gi
            b = pr * gi - pi * gr
            re, im = (a, b) if re is None else (re + a, im + b)
            at = rows_of(p, win)
            gprobe[pl.ds(at[0][m], win)] += o0r * gr + o0i * gi
            gprobe[pl.ds(at[1][m], win)] += o0r * gi - o0i * gr
        gobj[0, 0, s] += re
        gobj[0, 1, s] += im

    def one_hot(at, target):
        return jnp.where(at == target, 1.0, 0.0).astype(BF16)

    def place(lay):
        for s in range(scans):
            k = lax.broadcasted_iota(jnp.int32, (win, wide), 0) + (off_ref[0, 0, 1, s] - HALO)
            k = jnp.where(k < 0, k + wide, k)
            cols = one_hot(lax.broadcasted_iota(jnp.int32, (win, wide), 1), k)
            for part in range(2):
                for t, term in enumerate(split(gobj[lay, part, s])):
                    spread[t, pl.ds(s * win, win), pl.ds(part * wide, wide)] = dot(
                        term, cols
                    ).astype(BF16)
        rows = []
        for s in range(scans):
            j = lax.broadcasted_iota(jnp.int32, (tall, win), 1) + off_ref[0, 0, 0, s]
            rows.append(one_hot(lax.broadcasted_iota(jnp.int32, (tall, win), 0), j))
        rows = jnp.concatenate(rows, axis=1)
        for part in range(2):
            cut = pl.ds(part * wide, wide)
            acc[part, lay] = dot(rows, spread[0, :, cut]) + dot(rows, spread[1, :, cut])

    def grads_start(lay):
        edge_of = lambda ch: acc[ch, lay, :, pl.ds(tile, LANES)]
        er, el, fl, fr = edge_r.at[lay], edge_l.at[lay], from_l.at[lay], from_r.at[lay]
        er[...] = packed(edge_of, 0, tall, 2)
        el[...] = packed(edge_of, LANES - HALO, tall, 2)
        ss, rs = g_send.at[lay], g_recv.at[lay]
        return [
            send(acc.at[:, lay, head, body], from_bot.at[lay], ss, rs, 0, (up, my_c)),
            send(acc.at[:, lay, after, body], from_top.at[lay], ss, rs, 1, (down, my_c)),
            send(er.at[mid], fl.at[mid], ss, rs, 2, (my_r, rgt)),
            send(el.at[mid], fr.at[mid], ss, rs, 3, (my_r, lft)),
            send(er.at[head], fl.at[after], ss, rs, 4, (up, rgt)),
            send(er.at[after], fl.at[head], ss, rs, 5, (down, rgt)),
            send(el.at[head], fr.at[after], ss, rs, 6, (up, lft)),
            send(el.at[after], fr.at[head], ss, rs, 7, (down, lft)),
        ]

    def grads_end(lay, copies):
        grad_ref[:, lay] = acc[:, lay, mid, body]
        for copy in copies:
            copy.wait()
        grad_ref[:, lay, head, :] += from_top[lay]
        grad_ref[:, lay, tail, :] += from_bot[lay]
        for ref, first, cols in (
            (from_l, 0, pl.ds(0, LANES)),
            (from_r, LANES - HALO, pl.ds(tile - LANES, LANES)),
        ):
            for ch in range(2):
                at = lane(tall)
                block = unpacked(ref[lay], ch, first)
                block = jnp.where((at >= first) & (at < first + HALO), block, 0.0)
                grad_ref[ch, lay, :, cols] += block[HALO : HALO + tile]
                grad_ref[ch, lay, head, cols] += block[:HALO]
                grad_ref[ch, lay, tail, cols] += block[HALO + tile :]

    n_rows = gprobe.shape[0] // chunks
    half = n_rows // 2
    piece = half // group
    odd = lax.rem(my_c, 2)
    partner = (my_r, my_c + 1 - 2 * odd)
    place_in = my_r * n_half + my_c // 2

    def mate(k):
        other = lax.rem(place_in + k, group)
        return other, (other // n_half, 2 * lax.rem(other, n_half) + odd)

    def rows_at(start, size):
        return pl.ds(pl.multiple_of(start, piece), size)

    def wait_all(sem, ref):
        pltpu.make_async_copy(ref, ref, sem).wait()

    def owned(c, q):
        return rows_at(c * n_rows + odd * half + q * piece, piece)

    def pair_start(c):
        return send(
            gprobe.at[rows_at(c * n_rows + (1 - odd) * half, half)],
            half_in.at[c],
            pair_send,
            pair_recv,
            c,
            partner,
        )

    def scatter_start(c, copy):
        copy.wait()
        half_sum[c] = gprobe[rows_at(c * n_rows + odd * half, half)] + half_in[c]

        @pl.loop(1, group)
        def _(k):
            other, where = mate(k)
            send(
                half_sum.at[c, rows_at(other * piece, piece)],
                parts.at[c, rows_at((k - 1) * piece, piece)],
                rs_send,
                rs_recv,
                c,
                where,
            )

    def gather_start(c):
        wait_all(rs_recv.at[c], parts.at[c])
        value = half_sum[c, rows_at(place_in * piece, piece)]
        for k in range(group - 1):
            value = value + parts[c, pl.ds(k * piece, piece)]
        own = owned(c, place_in)
        total[own] = value

        @pl.loop(1, group)
        def _(k):
            pltpu.make_async_remote_copy(
                src_ref=total.at[own],
                dst_ref=total.at[own],
                send_sem=ag_send.at[c],
                recv_sem=ag_recv.at[c, k],
                device_id=mate(k)[1],
                device_id_type=MESH,
            ).start()

        send(total.at[own], total.at[own], fw_send, fw_recv, c, partner)

    def forward_start(c):
        @pl.loop(1, group)
        def _(k):
            got = total.at[owned(c, lax.rem(place_in + group - k, group))]
            wait_all(ag_recv.at[c, k], got)
            send(got, got, fw_send, fw_recv, c, partner)

    early = chunks == 2
    late = chunks - 1

    @pl.loop(0, scans)
    def _(s):
        first_half(0, s)
        second_half(0, s)

    pl.semaphore_wait(barrier, n_dev - 1)
    pair_0 = pair_start(0) if early else None

    @pl.loop(0, scans)
    def _(s):
        first_half(1, s)

    if early:
        scatter_start(0, pair_0)
    place(1)
    copies_1 = grads_start(1)

    @pl.loop(0, scans)
    def _(s):
        second_half(1, s)

    pair_1 = pair_start(late)
    place(0)
    scatter_start(late, pair_1)
    if early:
        gather_start(0)
    copies_0 = grads_start(0)
    grads_end(1, copies_1)
    gather_start(late)
    if early:
        forward_start(0)
    grads_end(0, copies_0)
    forward_start(late)
    for c in range(chunks):
        wait_all(fw_recv.at[c], half_in.at[c])
    full = total[...]
    scale = STEP_SIZE / jnp.sqrt(jnp.sum(full * full, keepdims=True) / full.size + EPSILON)
    for p in range(2):
        for part in range(2):
            for m in range(2):
                at = rows_of(p, win)[part][m]
                new_ref[part, 2 * p + m] = (
                    probe_ref[part, 2 * p + m] - scale * total[pl.ds(at, win)]
                )
    for c in range(chunks):
        wait_all(rs_send.at[c], parts.at[c])
        wait_all(ag_send.at[c], parts.at[c])
        wait_all(fw_send.at[c], half_in.at[c])


def on_device(object_tiles, probe_modes, offsets, amplitude):
    n_row, n_col = lax.axis_size("row"), lax.axis_size("col")
    n_dev = n_row * n_col
    tile, win, scans = object_tiles.shape[2], probe_modes.shape[2], offsets.shape[2]
    tall, wide = tile + 2 * HALO, tile + LANES
    g_rows = 2 * probe_modes.shape[1] * win
    chunks = 2 if g_rows // 2 % (8 * n_dev) == 0 else 1
    half = g_rows // chunks // 2
    group = n_dev // 2
    vmem = pl.BlockSpec(memory_space=pltpu.VMEM)
    smem = pl.BlockSpec(memory_space=pltpu.SMEM)
    dma = pltpu.SemaphoreType.DMA
    side = pltpu.VMEM((tall, LANES), F32)
    sides = pltpu.VMEM((2, tall, LANES), F32)
    wide_tile = jax.ShapeDtypeStruct((2, 2, tall + SUB, wide), F32)
    limit = 40 * 1024 * 1024
    pairs = offsets.transpose(0, 1, 3, 2)
    ext = pl.pallas_call(
        functools.partial(halo_kernel, (n_row, n_col)),
        out_shape=wide_tile,
        in_specs=[vmem],
        out_specs=vmem,
        scratch_shapes=[
            pltpu.VMEM((tile, LANES), F32),
            pltpu.VMEM((tile, LANES), F32),
            side,
            side,
            dma((8,)),
            dma((8,)),
        ],
        compiler_params=pltpu.CompilerParams(
            collective_id=0, has_side_effects=True, vmem_limit_bytes=limit
        ),
    )(object_tiles)
    winds = pl.pallas_call(
        functools.partial(window_kernel, (win, scans)),
        out_shape=jax.ShapeDtypeStruct((scans, 4, win, win), F32),
        in_specs=[smem, vmem],
        out_specs=vmem,
        compiler_params=pltpu.CompilerParams(vmem_limit_bytes=limit),
    )(pairs, ext)
    return pl.pallas_call(
        functools.partial(main_kernel, (n_row, n_col, win, scans, chunks)),
        out_shape=(
            jax.ShapeDtypeStruct(object_tiles.shape, F32),
            jax.ShapeDtypeStruct(probe_modes.shape, F32),
        ),
        in_specs=[smem] + [vmem] * 4,
        out_specs=(vmem, vmem),
        scratch_shapes=[
            pltpu.VMEM((scans, 2, 2 * win, 2 * win), F32),
            pltpu.VMEM((scans, 2, 2 * win, 2 * win), F32),
            pltpu.VMEM((scans, win, win), F32),
            pltpu.VMEM((2, 2, scans, win, win), F32),
            pltpu.VMEM((g_rows, win), F32),
            pltpu.VMEM((2, 2, tall, wide), F32),
            pltpu.VMEM((g_rows, win), F32),
            pltpu.VMEM((2, scans * win, 2 * wide), BF16),
            pltpu.VMEM((2, 2, HALO, tile), F32),
            pltpu.VMEM((2, 2, HALO, tile), F32),
            sides,
            sides,
            sides,
            sides,
            pltpu.VMEM((chunks, half, win), F32),
            pltpu.VMEM((chunks, half, win), F32),
            pltpu.VMEM((chunks, half - half // group, win), F32),
            dma((2, 8)),
            dma((2, 8)),
            dma((chunks,)),
            dma((chunks,)),
            dma((chunks,)),
            dma((chunks,)),
            dma((chunks,)),
            dma((chunks, group)),
            dma((chunks,)),
            dma((chunks,)),
        ],
        compiler_params=pltpu.CompilerParams(
            collective_id=1, has_side_effects=True, vmem_limit_bytes=limit
        ),
    )(pairs, winds, probe_modes, amplitude, jnp.asarray(tables(win)))


def solution(mesh):
    placed = (
        P(None, None, "row", "col"),
        P(),
        P("row", "col", None, None),
        P("row", "col", None, None, None),
    )
    return jax.shard_map(
        on_device,
        mesh=mesh,
        in_specs=placed,
        out_specs=(P(None, None, "row", "col"), P()),
        check_vma=False,
    )
```

profile of v0, /device:TPU:0, one launch (start us, length us, event | category | flops | bytes accessed | tf_op | source)
XLA Modules:
  0.0 57.3 jit_solution(2343200479184111821)
XLA Ops:
  0.6 0.0 copy-start.4
  0.6 0.0 copy-start
  0.6 1.2 %copy-done = f32[2,2,256,256]{3,2,1,0:T(8,128)S(1)} copy-done((f32[2,2,256,256]{3,2,1,0:T(8,128)S(1)}, f32[2,2,256,256]{3,2,1,0:T(8,128)}, u32[]{:S(2)}) %copy-start) | copy-done | bytes 1048600
  1.9 13.6 %shard_map.68.ext = f32[2,2,328,384]{3,2,1,0:T(8,128)S(1)} custom-call(f32[2,2,256,256]{3,2,1,0:T(8,128)S(1)} %copy-done), custom_call_target="tpu_custom_call" | custom-call | tf_op jit(solution)/shard_map/pallas_call | solution.py:508
  15.5 0.0 copy-done.4
  15.5 0.0 copy-start.1
  15.5 0.0 copy-start.2
  15.5 0.0 copy-start.3
  15.5 1.5 %shard_map.69.winds = f32[3,4,128,128]{3,2,1,0:T(8,128)S(1)} custom-call(s32[1,1,2,3]{3,2,1,0:T(2,128)S(1)} %bitcast.1, f32[2,2,328,384]{3,2,1,0:T(8,128)S(1)} %shard_map.68.ext), custom_call_target="tpu_custom_call" | custom-call | tf_op jit(solution)/shard_map/pallas_call | solution.py:525
  17.0 0.0 copy-done.1
  17.0 0.0 copy-done.2
  17.0 0.0 copy-done.3
  17.0 38.5 %shard_map.70 = (f32[2,2,256,256]{3,2,1,0:T(8,128)S(1)}, f32[2,4,128,128]{3,2,1,0:T(8,128)S(1)}) custom-call(s32[1,1,2,3]{3,2,1,0:T(2,128)S(1)} %bitcast.2, f32[3,4,128,128]{3,2,1,0:T(8,128)S(1)} %shard_map.69.winds, f32[2,4,128,128]{3,2,1,0:T(8,128)S(1)} %copy-done.2, f32[1,1,3,128,128]{4,3,2,1,0:T(8,128)S(1)} %copy-done.3, bf16[8,256,256]{2,1,0:T(8,128)(2,1)S(1)} %copy-done.1), custom_call_target="tpu_custom_call" | custom-call | tf_op jit(solution)/shard_map/pallas_call | solution.py:532
  55.5 1.0 %copy.9 = f32[2,2,256,256]{3,2,1,0:T(8,128)} copy(f32[2,2,256,256]{3,2,1,0:T(8,128)S(1)} %get-tuple-element.4) | data formatting | bytes 2097152
  56.5 0.8 %copy.10 = f32[2,4,128,128]{3,2,1,0:T(8,128)} copy(f32[2,4,128,128]{3,2,1,0:T(8,128)S(1)} %get-tuple-element.5) | data formatting | bytes 1048576
Async XLA Ops:
  0.6 14.8 %copy-start.4 = (s32[1,1,3,2]{2,3,1,0:T(2,128)S(1)}, s32[1,1,3,2]{2,3,1,0:T(2,128)}, u32[]{:S(2)}) copy-start(s32[1,1,3,2]{2,3,1,0:T(2,128)} %param.7) | copy-start | bytes 76
  0.6 1.2 %copy-start = (f32[2,2,256,256]{3,2,1,0:T(8,128)S(1)}, f32[2,2,256,256]{3,2,1,0:T(8,128)}, u32[]{:S(2)}) copy-start(f32[2,2,256,256]{3,2,1,0:T(8,128)} %obj_ref.1) | copy-start | bytes 3145732
  15.5 1.5 %copy-start.1 = (bf16[8,256,256]{2,1,0:T(8,128)(2,1)S(1)}, bf16[8,256,256]{2,1,0:T(8,128)(2,1)}, u32[]{:S(2)}) copy-start(bf16[8,256,256]{2,1,0:T(8,128)(2,1)} %constant.2.clone.tab) | copy-start | bytes 3145732
  15.5 1.5 %copy-start.2 = (f32[2,4,128,128]{3,2,1,0:T(8,128)S(1)}, f32[2,4,128,128]{3,2,1,0:T(8,128)}, u32[]{:S(2)}) copy-start(f32[2,4,128,128]{3,2,1,0:T(8,128)} %probe_ref.1) | copy-start | bytes 1572868
  15.5 1.5 %copy-start.3 = (f32[1,1,3,128,128]{4,3,2,1,0:T(8,128)S(1)}, f32[1,1,3,128,128]{4,3,2,1,0:T(8,128)}, u32[]{:S(2)}) copy-start(f32[1,1,3,128,128]{4,3,2,1,0:T(8,128)} %amp_ref.1) | copy-start | bytes 589828
where the time goes:
time: 57.6 us; the launch traced here: 57.3 us
  Pallas kernels  53.5 us (93%)
  local copies, waits for them, and re-layouts  3.01 us (5%)
  between operations  0.73 us (1%)
    pallas_call x1, Pallas kernels, on_device(): pl.pallas_call(functools.partial(main_kernel, (n_row, n_col, win, scans,...  38.5 us
    pallas_call x1, Pallas kernels, on_device(): pl.pallas_call(functools.partial(halo_kernel, (n_row, n_col)), out_shape=...  13.6 us
    unnamed x12, local copies, waits for them, and re-layouts  3.01 us
    pallas_call x1, Pallas kernels, on_device(): pl.pallas_call(functools.partial(window_kernel, (win, scans)), out_shape=...  1.48 us

commit v1 on v0

v1 whole, which is shorter than its diff:
```python
import functools

import jax
import jax.numpy as jnp
import numpy as np
from jax import lax
from jax.experimental import pallas as pl
from jax.experimental.pallas import tpu as pltpu
from jax.sharding import PartitionSpec as P

HALO = 32
PROP = 0.002
SHIFT_AMP = 0.5
STEP_SIZE = 0.5
EPSILON = 1e-06
LANES = 128
SUB = 8
MESH = pl.DeviceIdType.MESH
F32 = jnp.float32
BF16 = jnp.bfloat16


def tables(win):
    k = np.arange(win)
    c = np.exp(-2j * np.pi * (k[:, None] * k[None, :] % win) / win) / np.sqrt(win)
    freq = (k + win // 2) % win - win // 2
    kern = np.conj(c) @ np.diag(np.exp(-1j * PROP * freq**2)) @ c
    out = []
    for m in (c, np.conj(c), kern, np.conj(kern)):
        full = np.block([[m.real, m.imag], [-m.imag, m.real]])
        high = full.astype(np.float32).astype(jnp.bfloat16)
        low = (full - high.astype(np.float64)).astype(np.float32).astype(jnp.bfloat16)
        out += [high, low]
    return np.stack(out)


FWD, INV, KER, KER_INV = 0, 1, 2, 3


def split(x):
    high = x.astype(BF16)
    return high, (x - high.astype(F32)).astype(BF16)


def dot(a, b):
    return jnp.dot(a, b, preferred_element_type=F32)


def right(x, tab, which):
    high, low = split(x)
    return dot(high, tab[2 * which]) + (
        dot(low, tab[2 * which]) + dot(high, tab[2 * which + 1])
    )


def left(x, tab, which):
    high, low = split(x)
    which = which ^ 1
    return dot(tab[2 * which], high) + (
        dot(tab[2 * which], low) + dot(tab[2 * which + 1], high)
    )


def swap(y):
    w = y.shape[0] // 2
    top = jnp.concatenate([y[:w, :w], y[w:, :w]], axis=1)
    low = jnp.concatenate([y[:w, w:], y[w:, w:]], axis=1)
    return jnp.concatenate([top, low], axis=0)


def twice(x, axis):
    return jnp.concatenate([x, x], axis=axis)


def lane(rows):
    return lax.broadcasted_iota(jnp.int32, (rows, LANES), 1)


FOLD = HALO // 2


def fold(get, rows, first):
    at = lane(rows // 2)
    out = None
    for part in range(2):
        x = get(part)
        for h in range(2):
            low = HALO * (2 * h + part)
            block = jnp.concatenate(
                [x[HALO * b + FOLD * h : HALO * b + FOLD * (h + 1)] for b in range(rows // HALO)],
                axis=0,
            )
            shift = (low - first) % LANES
            block = pltpu.roll(block, shift, 1) if shift else block
            keep = (at >= low) & (at < low + HALO)
            out = jnp.where(keep, block, 0.0 if out is None else out)
    return out


def unfold(x, part, first):
    halves = []
    for h in range(2):
        shift = (first - HALO * (2 * h + part)) % LANES
        halves.append(pltpu.roll(x, shift, 1) if shift else x)
    return jnp.concatenate(
        [
            halves[h][FOLD * b : FOLD * (b + 1)]
            for b in range(x.shape[0] // FOLD)
            for h in range(2)
        ],
        axis=0,
    )


def remote(src, dst, ssem, rsem, to):
    copy = pltpu.make_async_remote_copy(
        src_ref=src,
        dst_ref=dst,
        send_sem=ssem,
        recv_sem=rsem,
        device_id=to,
        device_id_type=MESH,
    )
    copy.start()
    return copy


def fused_kernel(
    sizes,
    off_ref,
    obj_hbm,
    probe_hbm,
    amp_hbm,
    tab_hbm,
    grad_ref,
    new_ref,
    ext_0,
    ext_1,
    probe,
    amp,
    tab,
    winds,
    wave,
    far,
    factor,
    gobj,
    gprobe,
    zpad,
    acc,
    pack_l,
    pack_r,
    halo_l,
    halo_r,
    from_top,
    from_bot,
    edge_l,
    edge_r,
    from_l,
    from_r,
    half_in,
    half_sum,
    r_parts,
    z_parts,
    total,
    in_sem,
    h_send,
    h_recv,
    g_send,
    g_recv,
    pair_send,
    pair_recv,
    r_send,
    r_recv,
    z_send,
    z_recv,
    ag_send,
    ag_recv,
    fw_send,
    fw_recv,
):
    n_row, n_col, win, scans, chunks = sizes
    n_z = n_col // 2
    ext = (ext_0, ext_1)
    tile = grad_ref.shape[2]
    tall = tile + 2 * HALO
    nt = tile // LANES
    pad = tall - win
    my_r, my_c = lax.axis_index("row"), lax.axis_index("col")

    def at(dr, dc):
        return lax.rem(my_r + dr % n_row, n_row), lax.rem(my_c + dc % n_col, n_col)

    loads = []
    for lay in range(2):
        for part in range(2):
            for t in range(nt):
                loads.append(
                    pltpu.make_async_copy(
                        obj_hbm.at[part, lay, :, pl.ds(t * LANES, LANES)],
                        ext[lay].at[part, t, pl.ds(HALO, tile), :],
                        in_sem.at[len(loads)],
                    )
                )
    per_lay = len(loads) // 2
    for src, dst in ((probe_hbm, probe), (tab_hbm, tab), (amp_hbm, amp)):
        loads.append(pltpu.make_async_copy(src, dst, in_sem.at[len(loads)]))
    for load in loads:
        load.start()
    barrier = pltpu.get_barrier_semaphore()
    mates = {(dr % n_row, dc % n_col) for dr in (-1, 0, 1) for dc in (-1, 0, 1)}
    mates |= {(k, 0) for k in range(n_row)} | {(0, 2 * k) for k in range(n_z)}
    mates.discard((0, 0))
    for mate in sorted(mates):
        pl.semaphore_signal(barrier, inc=1, device_id=at(*mate), device_id_type=MESH)

    head, tail = pl.ds(0, FOLD), pl.ds((tile - HALO) // 2, FOLD)
    mid, after = pl.ds(FOLD, tile // 2), pl.ds(FOLD + tile // 2, FOLD)

    def pack(lay):
        for load in loads[lay * per_lay : (lay + 1) * per_lay]:
            load.wait()
        own = pl.ds(HALO, tile)
        pack_l[lay] = fold(lambda part: ext[lay][part, 0, own, :], tile, 0)
        pack_r[lay] = fold(lambda part: ext[lay][part, nt - 1, own, :], tile, LANES - HALO)

    def halo_start(lay):
        e, left_in, right_in = ext[lay], halo_l.at[lay], halo_r.at[lay]
        pl_, pr_ = pack_l.at[lay], pack_r.at[lay]
        own = pl.ds(0, nt)
        plan = [
            (e.at[:, own, pl.ds(tile, HALO)], e.at[:, own, pl.ds(0, HALO)], (1, 0)),
            (e.at[:, own, pl.ds(HALO, HALO)], e.at[:, own, pl.ds(HALO + tile, HALO)], (-1, 0)),
            (pr_, left_in.at[mid], (0, 1)),
            (pl_, right_in.at[mid], (0, -1)),
            (pr_.at[tail], left_in.at[head], (1, 1)),
            (pr_.at[head], left_in.at[after], (-1, 1)),
            (pl_.at[tail], right_in.at[head], (1, -1)),
            (pl_.at[head], right_in.at[after], (-1, -1)),
        ]
        return [
            remote(src, dst, h_send.at[lay, i], h_recv.at[lay, i], at(*to))
            for i, (src, dst, to) in enumerate(plan)
        ]

    def halo_end(lay, copies):
        for copy in copies:
            copy.wait_recv()
        for part in range(2):
            near = unfold(halo_r[lay], part, 0)
            distant = unfold(halo_l[lay], part, LANES - HALO)
            x = lane(tall)
            ext[lay][part, nt, pl.ds(0, tall), :] = jnp.where(
                x < HALO, near, jnp.where(x >= LANES - HALO, distant, 0.0)
            )

    def spot(s):
        row = off_ref[0, 0, 0, s]
        col = off_ref[0, 0, 1, s] - HALO
        col = jnp.where(col < 0, col + (nt + 1) * LANES, col)
        first = lax.div(col, LANES)
        second = jnp.where(first == nt, 0, first + 1)
        return row, first, second, col - first * LANES

    def windows(lay):
        @pl.loop(0, scans)
        def _(s):
            row, first, second, rem = spot(s)
            for part in range(2):
                a = ext[lay][part, first, pl.ds(row, win), :]
                b = ext[lay][part, second, pl.ds(row, win), :]
                block = jnp.where(lane(win) >= rem, a, b)
                winds[s, 2 * part + lay] = pltpu.roll(block, lax.rem(LANES - rem, LANES), 1)

    pack(0)
    pl.semaphore_wait(barrier, len(mates))
    halo_0 = halo_start(0)
    pack(1)
    halo_1 = halo_start(1)
    gprobe[...] = jnp.zeros_like(gprobe)
    gobj[...] = jnp.zeros_like(gobj)
    zpad[...] = jnp.zeros_like(zpad)
    for load in loads[2 * per_lay :]:
        load.wait()
    halo_end(0, halo_0)
    windows(0)

    @pl.loop(0, scans)
    def _(s):
        or_, oi_ = winds[s, 0], winds[s, 2]
        for p in range(2):
            rows = []
            for m in range(2):
                pr, pi = probe[0, 2 * p + m], probe[1, 2 * p + m]
                rows.append(
                    jnp.concatenate([pr * or_ - pi * oi_, pr * oi_ + pi * or_], axis=1)
                )
            psi = jnp.concatenate(rows, axis=0)
            wave[s, p] = left(swap(right(psi, tab, KER)), tab, KER)

    halo_end(1, halo_1)
    windows(1)

    @pl.loop(0, scans)
    def _(s):
        power = None
        for p in range(2):
            w = wave[s, p]
            wr, wi = w[:win], w[win:]
            o1r, o1i = twice(winds[s, 1], 1), twice(winds[s, 3], 1)
            psi = jnp.concatenate([wr * o1r - wi * o1i, wr * o1i + wi * o1r], axis=0)
            psi = right(swap(left(psi, tab, FWD)), tab, FWD)
            far[s, p] = psi
            sq = psi * psi
            part_sum = (sq[:win, :win] + sq[:win, win:]) + (sq[win:, :win] + sq[win:, win:])
            power = part_sum if power is None else power + part_sum
        root = jnp.sqrt(power + SHIFT_AMP)
        factor[s] = 2.0 * (root - amp[0, 0, s]) / root

    def first_half(p, s):
        g = far[s, p] * twice(twice(factor[s], 0), 1)
        g = left(swap(right(g, tab, INV)), tab, INV)
        w = wave[s, p]
        gr, gi, wr, wi = g[:win], g[win:], w[:win], w[win:]
        re = wr * gr + wi * gi
        im = wr * gi - wi * gr
        gobj[1, 0, s] += re[:, :win] + re[:, win:]
        gobj[1, 1, s] += im[:, :win] + im[:, win:]
        o1r, o1i = twice(winds[s, 1], 1), twice(winds[s, 3], 1)
        far[s, p] = jnp.concatenate([o1r * gr + o1i * gi, o1r * gi - o1i * gr], axis=0)

    def second_half(p, s):
        g = right(swap(left(far[s, p], tab, KER_INV)), tab, KER_INV)
        o0r, o0i = winds[s, 0], winds[s, 2]
        re = im = None
        for m in range(2):
            gr, gi = g[m * win : (m + 1) * win, :win], g[m * win : (m + 1) * win, win:]
            pr, pi = probe[0, 2 * p + m], probe[1, 2 * p + m]
            a = pr * gr + pi * gi
            b = pr * gi - pi * gr
            re, im = (a, b) if re is None else (re + a, im + b)
            base = (2 * p + m) * 2 * win
            gprobe[pl.ds(base, win)] += o0r * gr + o0i * gi
            gprobe[pl.ds(base + win, win)] += o0r * gi - o0i * gr
        gobj[0, 0, s] += re
        gobj[0, 1, s] += im

    def place(lay):
        starts = []
        for s in range(scans):
            row, first, second, rem = spot(s)
            starts.append(pad - row)
            where = jnp.where(lane(win) >= rem, first, second)
            for part in range(2):
                block = pltpu.roll(gobj[lay, part, s], rem, 1)
                for t in range(nt + 1):
                    zpad[s, part, t, pl.ds(pad, win), :] = jnp.where(where == t, block, 0.0)
        for part in range(2):
            for t in range(nt + 1):
                value = None
                for s in range(scans):
                    block = zpad[s, part, t, pl.ds(starts[s], tall), :]
                    value = block if value is None else value + block
                acc[lay, part, t] = value

    def grads_start(lay):
        a, er, el = acc.at[lay], edge_r.at[lay], edge_l.at[lay]
        fl, fr = from_l.at[lay], from_r.at[lay]
        edge_r[lay] = fold(lambda part: acc[lay, part, nt], tall, 0)
        edge_l[lay] = fold(lambda part: acc[lay, part, nt], tall, LANES - HALO)
        own = pl.ds(0, nt)
        plan = [
            (a.at[:, own, pl.ds(0, HALO)], from_bot.at[lay], (-1, 0)),
            (a.at[:, own, pl.ds(HALO + tile, HALO)], from_top.at[lay], (1, 0)),
            (er.at[mid], fl.at[mid], (0, 1)),
            (el.at[mid], fr.at[mid], (0, -1)),
            (er.at[head], fl.at[after], (-1, 1)),
            (er.at[after], fl.at[head], (1, 1)),
            (el.at[head], fr.at[after], (-1, -1)),
            (el.at[after], fr.at[head], (1, -1)),
        ]
        return [
            remote(src, dst, g_send.at[lay, i], g_recv.at[lay, i], at(*to))
            for i, (src, dst, to) in enumerate(plan)
        ]

    def grads_end(lay, copies):
        for copy in copies:
            copy.wait_recv()
        x = lane(tall)
        for part in range(2):
            for t in range(nt):
                value = acc[lay, part, t, pl.ds(HALO, tile), :]
                top, bot = from_top[lay, part, t], from_bot[lay, part, t]
                for ref, first, edge in ((from_l, 0, 0), (from_r, LANES - HALO, nt - 1)):
                    if t == edge:
                        block = unfold(ref[lay], part, first)
                        block = jnp.where((x >= first) & (x < first + HALO), block, 0.0)
                        value = value + block[HALO : HALO + tile]
                        top = top + block[:HALO]
                        bot = bot + block[HALO + tile :]
                cols = pl.ds(t * LANES, LANES)
                grad_ref[part, lay, pl.ds(0, HALO), cols] = value[:HALO] + top
                grad_ref[part, lay, pl.ds(HALO, tile - 2 * HALO), cols] = value[HALO:-HALO]
                grad_ref[part, lay, pl.ds(tile - HALO, HALO), cols] = value[-HALO:] + bot

    odd = lax.rem(my_c, 2)
    partner = (my_r, my_c + 1 - 2 * odd)
    my_z = lax.div(my_c, 2)

    def span(c):
        start, size = chunks[c]
        half = size // 2
        piece = half // n_row
        return start, half, piece, start // 2, start // 2 // n_row

    def rows_at(start, size):
        return pl.ds(pl.multiple_of(start, SUB), size)

    def row_mate(k):
        return lax.rem(my_r + k, n_row)

    def pair_start(c):
        start, half, piece, hs, ps = span(c)
        return remote(
            gprobe.at[rows_at(start + (1 - odd) * half, half)],
            half_in.at[pl.ds(hs, half)],
            pair_send.at[c],
            pair_recv.at[c],
            partner,
        )

    def r_start(c, pair):
        start, half, piece, hs, ps = span(c)
        pair.wait_recv()
        half_sum[pl.ds(hs, half)] = (
            gprobe[rows_at(start + odd * half, half)] + half_in[pl.ds(hs, half)]
        )
        copies = []
        for k in range(1, n_row):
            q = row_mate(k)
            copies.append(
                remote(
                    half_sum.at[rows_at(hs + q * piece, piece)],
                    r_parts.at[k - 1, pl.ds(ps, piece)],
                    r_send.at[c, k - 1],
                    r_recv.at[c, k - 1],
                    (q, my_c),
                )
            )
        return copies

    def z_start(c, before):
        start, half, piece, hs, ps = span(c)
        for copy in before:
            copy.wait_recv()
        value = half_sum[rows_at(hs + my_r * piece, piece)]
        for k in range(n_row - 1):
            value = value + r_parts[k, pl.ds(ps, piece)]
        z_parts[my_z, pl.ds(ps, piece)] = value
        mine = z_parts.at[my_z, pl.ds(ps, piece)]
        return [
            remote(mine, mine, z_send.at[c, k - 1], z_recv.at[c, k - 1], at(0, 2 * k))
            for k in range(1, n_z)
        ]

    def ag_start(c, before):
        start, half, piece, hs, ps = span(c)
        for copy in before:
            copy.wait_recv()
        value = z_parts[0, pl.ds(ps, piece)]
        for k in range(1, n_z):
            value = value + z_parts[k, pl.ds(ps, piece)]
        own = rows_at(start + odd * half + my_r * piece, piece)
        total[own] = value
        mine = total.at[own]
        copies = [
            remote(mine, mine, ag_send.at[c, k - 1], ag_recv.at[c, k - 1], at(k, 0))
            for k in range(1, n_row)
        ]
        return copies, [remote(mine, mine, fw_send.at[c, 0], fw_recv.at[c, 0], partner)]

    def fw_start(c, copies, forwards):
        start, half, piece, hs, ps = span(c)
        for k in range(1, n_row):
            copies[k - 1].wait_recv()
            q = lax.rem(my_r + n_row - k, n_row)
            got = total.at[rows_at(start + odd * half + q * piece, piece)]
            forwards.append(remote(got, got, fw_send.at[c, k], fw_recv.at[c, k], partner))

    @pl.loop(0, scans)
    def _(s):
        first_half(0, s)
        second_half(0, s)

    early, late = range(len(chunks) // 2), range(len(chunks) // 2, len(chunks))
    every = range(len(chunks))
    pair, row, zed, gat = {}, {}, {}, {}
    for c in early:
        pair[c] = pair_start(c)

    @pl.loop(0, scans)
    def _(s):
        first_half(1, s)

    for c in early:
        row[c] = r_start(c, pair[c])
    place(1)
    copies_1 = grads_start(1)

    @pl.loop(0, scans)
    def _(s):
        second_half(1, s)

    for c in late:
        pair[c] = pair_start(c)
    place(0)
    for c in late:
        row[c] = r_start(c, pair[c])
    copies_0 = grads_start(0)
    for c in early:
        zed[c] = z_start(c, row[c])
    for c in late:
        zed[c] = z_start(c, row[c])
    grads_end(1, copies_1)
    for c in every:
        gat[c] = ag_start(c, zed[c])
    grads_end(0, copies_0)
    for c in every:
        fw_start(c, *gat[c])
    for c in every:
        for copy in gat[c][1]:
            copy.wait_recv()
    full = total[...]
    scale = STEP_SIZE / jnp.sqrt(jnp.sum(full * full, keepdims=True) / full.size + EPSILON)
    for m in range(probe.shape[1]):
        for part in range(2):
            new_ref[part, m] = (
                probe[part, m] - scale * total[pl.ds((2 * m + part) * win, win)]
            )
    for copy in halo_0 + halo_1 + copies_0 + copies_1:
        copy.wait_send()
    for c in every:
        for copy in [pair[c]] + row[c] + zed[c] + gat[c][0] + gat[c][1]:
            copy.wait_send()


def out_kernel(grad, new, grad_out, new_out, sem):
    copies = []
    for part in range(2):
        for lay in range(grad.shape[1]):
            copies.append((grad.at[part, lay], grad_out.at[part, lay]))
        copies.append((new.at[part], new_out.at[part]))
    copies = [
        pltpu.make_async_copy(src, dst, sem.at[i]) for i, (src, dst) in enumerate(copies)
    ]
    for copy in copies:
        copy.start()
    for copy in copies:
        copy.wait()


def on_device(object_tiles, probe_modes, offsets, amplitude):
    n_row, n_col = lax.axis_size("row"), lax.axis_size("col")
    n_z = n_col // 2
    tile, win, scans = object_tiles.shape[2], probe_modes.shape[2], offsets.shape[2]
    tall, nt = tile + 2 * HALO, tile // LANES
    modes = probe_modes.shape[1]
    g_rows = 2 * modes * win
    size = g_rows // CHUNKS
    chunks = tuple((i * size, size) for i in range(CHUNKS))
    piece = g_rows // 2 // n_row
    vmem = pl.BlockSpec(memory_space=pltpu.VMEM)
    smem = pl.BlockSpec(memory_space=pltpu.SMEM)
    hbm = pl.BlockSpec(memory_space=pltpu.HBM)
    dma = pltpu.SemaphoreType.DMA
    block = lambda *shape: pltpu.VMEM(shape, F32)
    pairs = offsets.transpose(0, 1, 3, 2)
    table = jnp.asarray(tables(win))
    grad, new = pl.pallas_call(
        functools.partial(fused_kernel, (n_row, n_col, win, scans, chunks)),
        out_shape=(
            jax.ShapeDtypeStruct(object_tiles.shape, F32),
            jax.ShapeDtypeStruct(probe_modes.shape, F32),
        ),
        in_specs=[smem] + [hbm] * 4,
        out_specs=(vmem, vmem),
        scratch_shapes=[
            block(2, nt + 1, tall, LANES),
            block(2, nt + 1, tall, LANES),
            block(*probe_modes.shape),
            block(*amplitude.shape),
            pltpu.VMEM(table.shape, BF16),
            block(scans, 4, win, win),
            block(scans, 2, 2 * win, 2 * win),
            block(scans, 2, 2 * win, 2 * win),
            block(scans, win, win),
            block(2, 2, scans, win, win),
            block(g_rows, win),
            block(scans, 2, nt + 1, 2 * tall - win, LANES),
            block(2, 2, nt + 1, tall, LANES),
            block(2, tile // 2, LANES),
            block(2, tile // 2, LANES),
            block(2, tall // 2, LANES),
            block(2, tall // 2, LANES),
            block(2, 2, nt, HALO, LANES),
            block(2, 2, nt, HALO, LANES),
            block(2, tall // 2, LANES),
            block(2, tall // 2, LANES),
            block(2, tall // 2, LANES),
            block(2, tall // 2, LANES),
            block(g_rows // 2, win),
            block(g_rows // 2, win),
            block(n_row - 1, piece, win),
            block(n_z, piece, win),
            block(g_rows, win),
            dma((4 * nt + 3,)),
            dma((2, 8)),
            dma((2, 8)),
            dma((2, 8)),
            dma((2, 8)),
            dma((CHUNKS,)),
            dma((CHUNKS,)),
            dma((CHUNKS, n_row - 1)),
            dma((CHUNKS, n_row - 1)),
            dma((CHUNKS, n_z - 1)),
            dma((CHUNKS, n_z - 1)),
            dma((CHUNKS, n_row - 1)),
            dma((CHUNKS, n_row - 1)),
            dma((CHUNKS, n_row)),
            dma((CHUNKS, n_row)),
        ],
        compiler_params=pltpu.CompilerParams(
            collective_id=0, has_side_effects=True, vmem_limit_bytes=48 * 1024 * 1024
        ),
    )(pairs, object_tiles, probe_modes, amplitude, table)
    return pl.pallas_call(
        out_kernel,
        out_shape=(
            jax.ShapeDtypeStruct(object_tiles.shape, F32),
            jax.ShapeDtypeStruct(probe_modes.shape, F32),
        ),
        in_specs=[vmem, vmem],
        out_specs=(hbm, hbm),
        scratch_shapes=[dma((6,))],
    )(grad, new)


CHUNKS = 2


def solution(mesh):
    placed = (
        P(None, None, "row", "col"),
        P(),
        P("row", "col", None, None),
        P("row", "col", None, None, None),
    )
    return jax.shard_map(
        on_device,
        mesh=mesh,
        in_specs=placed,
        out_specs=(P(None, None, "row", "col"), P()),
        check_vma=False,
    )
```

time: 57.6 us -> 55.3 us (0.960)
  Pallas kernels: 53.5 us -> 47.2 us
  local copies, waits for them, and re-layouts: 3.01 us -> 6.86 us
    pallas_call x3 -> x2, Pallas kernels: 53.5 us -> 47.2 us  [the longest x1 44.7 us: on_device(): pl.pallas_call(functools.partial(fused_kernel, (n_row, n_col, win, scans,...]
    unnamed x12 -> x14, local copies, waits for them, and re-layouts: 3.01 us -> 6.86 us
where the time goes in v1:
time: 55.3 us; the launch traced here: 54.7 us
  Pallas kernels  47.2 us (85%)
  local copies, waits for them, and re-layouts  6.86 us (12%)
  between operations  0.66 us (1%)
    pallas_call x1, Pallas kernels, on_device(): pl.pallas_call(functools.partial(fused_kernel, (n_row, n_col, win, scans,...  44.7 us
    unnamed x14, local copies, waits for them, and re-layouts  6.86 us
    pallas_call x1, Pallas kernels, on_device(): pl.pallas_call(out_kernel, out_shape=(jax.ShapeDtypeStruct(object_tiles.s...  2.54 us

profile of v1, /device:TPU:0, one launch (start us, length us, event | category | flops | bytes accessed | tf_op | source)
XLA Modules:
  0.0 54.7 jit_solution(10862841028937989970)
XLA Ops:
  0.6 0.0 copy-start.6
  0.6 0.7 %copy-done.6 = s32[1,1,3,2]{2,3,1,0:T(2,128)S(1)} copy-done((s32[1,1,3,2]{2,3,1,0:T(2,128)S(1)}, s32[1,1,3,2]{2,3,1,0:T(2,128)}, u32[]{:S(2)}) %copy-start.6) | copy-done | bytes 48
  1.3 0.0 copy-start
  1.3 1.2 %copy-done = f32[2,2,256,256]{3,2,1,0:T(8,128)S(1)} copy-done((f32[2,2,256,256]{3,2,1,0:T(8,128)S(1)}, f32[2,2,256,256]{3,2,1,0:T(8,128)}, u32[]{:S(2)}) %copy-start) | copy-done | bytes 1048600
  2.5 0.0 copy-start.1
  2.5 1.2 %copy-done.1 = bf16[8,256,256]{2,1,0:T(8,128)(2,1)S(1)} copy-done((bf16[8,256,256]{2,1,0:T(8,128)(2,1)S(1)}, bf16[8,256,256]{2,1,0:T(8,128)(2,1)}, u32[]{:S(2)}) %copy-start.1) | copy-done | bytes 1048600
  3.8 0.0 copy-start.3
  3.8 1.0 %copy-done.3 = f32[2,4,128,128]{3,2,1,0:T(8,128)S(1)} copy-done((f32[2,4,128,128]{3,2,1,0:T(8,128)S(1)}, f32[2,4,128,128]{3,2,1,0:T(8,128)}, u32[]{:S(2)}) %copy-start.3) | copy-done | bytes 524312
  4.8 0.0 copy-start.5
  4.8 0.9 %copy-done.5 = f32[1,1,3,128,128]{4,3,2,1,0:T(8,128)S(1)} copy-done((f32[1,1,3,128,128]{4,3,2,1,0:T(8,128)S(1)}, f32[1,1,3,128,128]{4,3,2,1,0:T(8,128)}, u32[]{:S(2)}) %copy-start.5) | copy-done | bytes 196632
  5.7 44.7 %shard_map.68 = (f32[2,2,256,256]{3,2,1,0:T(8,128)S(1)}, f32[2,4,128,128]{3,2,1,0:T(8,128)S(1)}) custom-call(s32[1,1,2,3]{3,2,1,0:T(2,128)S(1)} %bitcast.1, f32[2,2,256,256]{3,2,1,0:T(8,128)S(1)} %copy-done, f32[2,4,128,128]{3,2,1,0:T(8,128)S(1)} %copy-done.3, f32[1,1,3,128,128]{4,3,2,1,0:T(8,128)S(1)} %copy-done.5, bf16[8,256,256]{2,1,0:T(8,128)(2,1)S(1)} %copy-done.1), custom_call_target="tpu_custom_call" | custom-call | tf_op jit(solution)/shard_map/pallas_call | solution.py:579
  50.4 0.0 copy-start.2
  50.4 1.0 %copy-done.2 = f32[2,2,256,256]{3,2,1,0:T(8,128)} copy-done((f32[2,2,256,256]{3,2,1,0:T(8,128)}, f32[2,2,256,256]{3,2,1,0:T(8,128)S(1)}, u32[]{:S(2)}) %copy-start.2) | copy-done | bytes 1048600
  51.4 0.0 copy-start.4
  51.4 0.8 %copy-done.4 = f32[2,4,128,128]{3,2,1,0:T(8,128)} copy-done((f32[2,4,128,128]{3,2,1,0:T(8,128)}, f32[2,4,128,128]{3,2,1,0:T(8,128)S(1)}, u32[]{:S(2)}) %copy-start.4) | copy-done | bytes 524312
  52.2 2.5 %shard_map.69 = (f32[2,2,256,256]{3,2,1,0:T(8,128)}, f32[2,4,128,128]{3,2,1,0:T(8,128)}) custom-call(f32[2,2,256,256]{3,2,1,0:T(8,128)} %copy-done.2, f32[2,4,128,128]{3,2,1,0:T(8,128)} %copy-done.4), custom_call_target="tpu_custom_call" | custom-call | tf_op jit(solution)/shard_map/pallas_call | solution.py:636
Async XLA Ops:
  0.6 0.7 %copy-start.6 = (s32[1,1,3,2]{2,3,1,0:T(2,128)S(1)}, s32[1,1,3,2]{2,3,1,0:T(2,128)}, u32[]{:S(2)}) copy-start(s32[1,1,3,2]{2,3,1,0:T(2,128)} %param.7) | copy-start | bytes 76
  1.3 1.2 %copy-start = (f32[2,2,256,256]{3,2,1,0:T(8,128)S(1)}, f32[2,2,256,256]{3,2,1,0:T(8,128)}, u32[]{:S(2)}) copy-start(f32[2,2,256,256]{3,2,1,0:T(8,128)} %obj_hbm.1) | copy-start | bytes 3145732
  2.5 1.2 %copy-start.1 = (bf16[8,256,256]{2,1,0:T(8,128)(2,1)S(1)}, bf16[8,256,256]{2,1,0:T(8,128)(2,1)}, u32[]{:S(2)}) copy-start(bf16[8,256,256]{2,1,0:T(8,128)(2,1)} %constant.2.clone.tab_hbm) | copy-start | bytes 3145732
  3.8 1.0 %copy-start.3 = (f32[2,4,128,128]{3,2,1,0:T(8,128)S(1)}, f32[2,4,128,128]{3,2,1,0:T(8,128)}, u32[]{:S(2)}) copy-start(f32[2,4,128,128]{3,2,1,0:T(8,128)} %probe_hbm.1) | copy-start | bytes 1572868
  4.8 0.9 %copy-start.5 = (f32[1,1,3,128,128]{4,3,2,1,0:T(8,128)S(1)}, f32[1,1,3,128,128]{4,3,2,1,0:T(8,128)}, u32[]{:S(2)}) copy-start(f32[1,1,3,128,128]{4,3,2,1,0:T(8,128)} %amp_hbm.1) | copy-start | bytes 589828
  50.4 1.0 %copy-start.2 = (f32[2,2,256,256]{3,2,1,0:T(8,128)}, f32[2,2,256,256]{3,2,1,0:T(8,128)S(1)}, u32[]{:S(2)}) copy-start(f32[2,2,256,256]{3,2,1,0:T(8,128)S(1)} %get-tuple-element.4.grad) | copy-start | bytes 3145732
  51.4 0.8 %copy-start.4 = (f32[2,4,128,128]{3,2,1,0:T(8,128)}, f32[2,4,128,128]{3,2,1,0:T(8,128)S(1)}, u32[]{:S(2)}) copy-start(f32[2,4,128,128]{3,2,1,0:T(8,128)S(1)} %get-tuple-element.5.new) | copy-start | bytes 1572868

commit v2 on v1

--- a/solution.py
+++ b/solution.py
@@ -127,13 +127,14 @@
 
 def fused_kernel(
     sizes,
-    off_ref,
+    off_hbm,
     obj_hbm,
     probe_hbm,
     amp_hbm,
     tab_hbm,
     grad_ref,
     new_ref,
+    off_ref,
     ext_0,
     ext_1,
     probe,
@@ -190,6 +191,12 @@
     def at(dr, dc):
         return lax.rem(my_r + dr % n_row, n_row), lax.rem(my_c + dc % n_col, n_col)
 
+    barrier = pltpu.get_barrier_semaphore()
+    mates = {(dr % n_row, dc % n_col) for dr in (-1, 0, 1) for dc in (-1, 0, 1)}
+    mates |= {(k, 0) for k in range(n_row)} | {(0, 2 * k) for k in range(n_z)}
+    mates.discard((0, 0))
+    for mate in sorted(mates):
+        pl.semaphore_signal(barrier, inc=1, device_id=at(*mate), device_id_type=MESH)
     loads = []
     for lay in range(2):
         for part in range(2):
@@ -202,16 +209,10 @@
                     )
                 )
     per_lay = len(loads) // 2
-    for src, dst in ((probe_hbm, probe), (tab_hbm, tab), (amp_hbm, amp)):
+    for src, dst in ((off_hbm, off_ref), (probe_hbm, probe), (tab_hbm, tab), (amp_hbm, amp)):
         loads.append(pltpu.make_async_copy(src, dst, in_sem.at[len(loads)]))
     for load in loads:
         load.start()
-    barrier = pltpu.get_barrier_semaphore()
-    mates = {(dr % n_row, dc % n_col) for dr in (-1, 0, 1) for dc in (-1, 0, 1)}
-    mates |= {(k, 0) for k in range(n_row)} | {(0, 2 * k) for k in range(n_z)}
-    mates.discard((0, 0))
-    for mate in sorted(mates):
-        pl.semaphore_signal(barrier, inc=1, device_id=at(*mate), device_id_type=MESH)
 
     head, tail = pl.ds(0, FOLD), pl.ds((tile - HALO) // 2, FOLD)
     mid, after = pl.ds(FOLD, tile // 2), pl.ds(FOLD + tile // 2, FOLD)
@@ -284,8 +285,7 @@
     halo_end(0, halo_0)
     windows(0)
 
-    @pl.loop(0, scans)
-    def _(s):
+    for s in range(scans):
         or_, oi_ = winds[s, 0], winds[s, 2]
         for p in range(2):
             rows = []
@@ -300,8 +300,7 @@
     halo_end(1, halo_1)
     windows(1)
 
-    @pl.loop(0, scans)
-    def _(s):
+    for s in range(scans):
         power = None
         for p in range(2):
             w = wave[s, p]
@@ -487,9 +486,9 @@
             got = total.at[rows_at(start + odd * half + q * piece, piece)]
             forwards.append(remote(got, got, fw_send.at[c, k], fw_recv.at[c, k], partner))
 
-    @pl.loop(0, scans)
-    def _(s):
+    for s in range(scans):
         first_half(0, s)
+    for s in range(scans):
         second_half(0, s)
 
     early, late = range(len(chunks) // 2), range(len(chunks) // 2, len(chunks))
@@ -498,8 +497,7 @@
     for c in early:
         pair[c] = pair_start(c)
 
-    @pl.loop(0, scans)
-    def _(s):
+    for s in range(scans):
         first_half(1, s)
 
     for c in early:
@@ -507,8 +505,7 @@
     place(1)
     copies_1 = grads_start(1)
 
-    @pl.loop(0, scans)
-    def _(s):
+    for s in range(scans):
         second_half(1, s)
 
     for c in late:
@@ -570,7 +567,6 @@
     chunks = tuple((i * size, size) for i in range(CHUNKS))
     piece = g_rows // 2 // n_row
     vmem = pl.BlockSpec(memory_space=pltpu.VMEM)
-    smem = pl.BlockSpec(memory_space=pltpu.SMEM)
     hbm = pl.BlockSpec(memory_space=pltpu.HBM)
     dma = pltpu.SemaphoreType.DMA
     block = lambda *shape: pltpu.VMEM(shape, F32)
@@ -582,9 +578,10 @@
             jax.ShapeDtypeStruct(object_tiles.shape, F32),
             jax.ShapeDtypeStruct(probe_modes.shape, F32),
         ),
-        in_specs=[smem] + [hbm] * 4,
+        in_specs=[hbm] * 5,
         out_specs=(vmem, vmem),
         scratch_shapes=[
+            pltpu.SMEM(pairs.shape, jnp.int32),
             block(2, nt + 1, tall, LANES),
             block(2, nt + 1, tall, LANES),
             block(*probe_modes.shape),
@@ -613,7 +610,7 @@
             block(n_row - 1, piece, win),
             block(n_z, piece, win),
             block(g_rows, win),
-            dma((4 * nt + 3,)),
+            dma((4 * nt + 4,)),
             dma((2, 8)),
             dma((2, 8)),
             dma((2, 8)),
@@ -632,7 +629,12 @@
         compiler_params=pltpu.CompilerParams(
             collective_id=0, has_side_effects=True, vmem_limit_bytes=48 * 1024 * 1024
         ),
-    )(pairs, object_tiles, probe_modes, amplitude, table)
+    )(
+        *[
+            pltpu.with_memory_space_constraint(x, pltpu.HBM)
+            for x in (pairs, object_tiles, probe_modes, amplitude, table)
+        ],
+    )
     return pl.pallas_call(
         out_kernel,
         out_shape=(
@@ -642,6 +644,7 @@
         in_specs=[vmem, vmem],
         out_specs=(hbm, hbm),
         scratch_shapes=[dma((6,))],
+        compiler_params=pltpu.CompilerParams(vmem_limit_bytes=1024 * 1024),
     )(grad, new)
 
 

time: 55.3 us -> 40.6 us (0.73)
  Pallas kernels: 47.2 us -> 39.6 us
  local copies, waits for them, and re-layouts: 6.86 us -> 0 us
    unnamed x14 -> x0, local copies, waits for them, and re-layouts: 6.86 us -> none
    pallas_call x1, Pallas kernels: 44.7 us -> 38.4 us  [on_device(): pl.pallas_call(functools.partial(fused_kernel, (n_row, n_col, win, scans,...]
    pallas_call x1, Pallas kernels: 2.54 us -> 1.19 us  [on_device(): pl.pallas_call(out_kernel, out_shape=(jax.ShapeDtypeStruct(object_tiles.s...]
where the time goes in v2:
time: 40.6 us; the launch traced here: 40.2 us
  Pallas kernels  39.6 us (98%)
  between operations  0.64 us (2%)
    pallas_call x1, Pallas kernels, on_device(): pl.pallas_call(functools.partial(fused_kernel, (n_row, n_col, win, scans,...  38.4 us
    pallas_call x1, Pallas kernels, on_device(): pl.pallas_call(out_kernel, out_shape=(jax.ShapeDtypeStruct(object_tiles.s...  1.19 us

profile of v2, /device:TPU:0, one launch (start us, length us, event | category | flops | bytes accessed | tf_op | source)
XLA Modules:
  0.0 40.2 jit_solution(8075913907899049466)
XLA Ops:
  0.6 38.4 %shard_map.68 = (f32[2,2,256,256]{3,2,1,0:T(8,128)S(1)}, f32[2,4,128,128]{3,2,1,0:T(8,128)S(1)}) custom-call(s32[1,1,2,3]{3,2,1,0:T(2,128)} %bitcast.1, f32[2,2,256,256]{3,2,1,0:T(8,128)} %obj_hbm.1, f32[2,4,128,128]{3,2,1,0:T(8,128)} %probe_hbm.1, f32[1,1,3,128,128]{4,3,2,1,0:T(8,128)} %amp_hbm.1, bf16[8,256,256]{2,1,0:T(8,128)(2,1)} %constant.2.clone.tab_hbm), custom_call_target="tpu_custom_call" | custom-call | tf_op jit(solution)/shard_map/pallas_call | solution.py:575
  39.0 1.2 %shard_map.69 = (f32[2,2,256,256]{3,2,1,0:T(8,128)}, f32[2,4,128,128]{3,2,1,0:T(8,128)}) custom-call(f32[2,2,256,256]{3,2,1,0:T(8,128)S(1)} %get-tuple-element.4.grad, f32[2,4,128,128]{3,2,1,0:T(8,128)S(1)} %get-tuple-element.5.new), custom_call_target="tpu_custom_call" | custom-call | tf_op jit(solution)/shard_map/pallas_call | solution.py:638

commit v3 on v2

--- a/solution.py
+++ b/solution.py
@@ -224,7 +224,7 @@
         pack_l[lay] = fold(lambda part: ext[lay][part, 0, own, :], tile, 0)
         pack_r[lay] = fold(lambda part: ext[lay][part, nt - 1, own, :], tile, LANES - HALO)
 
-    def halo_start(lay):
+    def halo_start(lay, which):
         e, left_in, right_in = ext[lay], halo_l.at[lay], halo_r.at[lay]
         pl_, pr_ = pack_l.at[lay], pack_r.at[lay]
         own = pl.ds(0, nt)
@@ -240,10 +240,10 @@
         ]
         return [
             remote(src, dst, h_send.at[lay, i], h_recv.at[lay, i], at(*to))
-            for i, (src, dst, to) in enumerate(plan)
+            for i, (src, dst, to) in ((i, plan[i]) for i in which)
         ]
 
-    def halo_end(lay, copies):
+    def halo_end(lay, copies, rows):
         for copy in copies:
             copy.wait_recv()
         for part in range(2):
@@ -253,6 +253,8 @@
             ext[lay][part, nt, pl.ds(0, tall), :] = jnp.where(
                 x < HALO, near, jnp.where(x >= LANES - HALO, distant, 0.0)
             )
+        for copy in rows:
+            copy.wait_recv()
 
     def spot(s):
         row = off_ref[0, 0, 0, s]
@@ -263,8 +265,7 @@
         return row, first, second, col - first * LANES
 
     def windows(lay):
-        @pl.loop(0, scans)
-        def _(s):
+        for s in range(scans):
             row, first, second, rem = spot(s)
             for part in range(2):
                 a = ext[lay][part, first, pl.ds(row, win), :]
@@ -272,17 +273,20 @@
                 block = jnp.where(lane(win) >= rem, a, b)
                 winds[s, 2 * part + lay] = pltpu.roll(block, lax.rem(LANES - rem, LANES), 1)
 
+    sides, ends = (4, 5, 6, 7, 2, 3), (0, 1)
     pack(0)
+    pack(1)
     pl.semaphore_wait(barrier, len(mates))
-    halo_0 = halo_start(0)
-    pack(1)
-    halo_1 = halo_start(1)
+    sides_0 = halo_start(0, sides)
+    sides_1 = halo_start(1, sides)
+    ends_0 = halo_start(0, ends)
+    ends_1 = halo_start(1, ends)
     gprobe[...] = jnp.zeros_like(gprobe)
     gobj[...] = jnp.zeros_like(gobj)
     zpad[...] = jnp.zeros_like(zpad)
     for load in loads[2 * per_lay :]:
         load.wait()
-    halo_end(0, halo_0)
+    halo_end(0, sides_0, ends_0)
     windows(0)
 
     for s in range(scans):
@@ -297,7 +301,7 @@
             psi = jnp.concatenate(rows, axis=0)
             wave[s, p] = left(swap(right(psi, tab, KER)), tab, KER)
 
-    halo_end(1, halo_1)
+    halo_end(1, sides_1, ends_1)
     windows(1)
 
     for s in range(scans):
@@ -361,11 +365,13 @@
                     value = block if value is None else value + block
                 acc[lay, part, t] = value
 
-    def grads_start(lay):
+    def grads_fold(lay):
+        edge_r[lay] = fold(lambda part: acc[lay, part, nt], tall, 0)
+        edge_l[lay] = fold(lambda part: acc[lay, part, nt], tall, LANES - HALO)
+
+    def grads_start(lay, which):
         a, er, el = acc.at[lay], edge_r.at[lay], edge_l.at[lay]
         fl, fr = from_l.at[lay], from_r.at[lay]
-        edge_r[lay] = fold(lambda part: acc[lay, part, nt], tall, 0)
-        edge_l[lay] = fold(lambda part: acc[lay, part, nt], tall, LANES - HALO)
         own = pl.ds(0, nt)
         plan = [
             (a.at[:, own, pl.ds(0, HALO)], from_bot.at[lay], (-1, 0)),
@@ -379,7 +385,7 @@
         ]
         return [
             remote(src, dst, g_send.at[lay, i], g_recv.at[lay, i], at(*to))
-            for i, (src, dst, to) in enumerate(plan)
+            for i, (src, dst, to) in ((i, plan[i]) for i in which)
         ]
 
     def grads_end(lay, copies):
@@ -486,47 +492,53 @@
             got = total.at[rows_at(start + odd * half + q * piece, piece)]
             forwards.append(remote(got, got, fw_send.at[c, k], fw_recv.at[c, k], partner))
 
+    early, late = range(len(chunks) // 2), range(len(chunks) // 2, len(chunks))
+    every = range(len(chunks))
+    pair, row, zed, gat = {}, {}, {}, {}
     for s in range(scans):
         first_half(0, s)
     for s in range(scans):
         second_half(0, s)
-
-    early, late = range(len(chunks) // 2), range(len(chunks) // 2, len(chunks))
-    every = range(len(chunks))
-    pair, row, zed, gat = {}, {}, {}, {}
     for c in early:
         pair[c] = pair_start(c)
-
     for s in range(scans):
         first_half(1, s)
-
+    place(1)
+    grads_fold(1)
+    copies_1 = grads_start(1, (4, 5, 6, 7, 2, 3))
     for c in early:
         row[c] = r_start(c, pair[c])
-    place(1)
-    copies_1 = grads_start(1)
-
     for s in range(scans):
         second_half(1, s)
-
     for c in late:
         pair[c] = pair_start(c)
     place(0)
+    grads_fold(0)
+    copies_0 = grads_start(0, (4, 5, 6, 7, 2, 3))
     for c in late:
         row[c] = r_start(c, pair[c])
-    copies_0 = grads_start(0)
+    copies_1 += grads_start(1, (0, 1))
+    copies_0 += grads_start(0, (0, 1))
     for c in early:
         zed[c] = z_start(c, row[c])
     for c in late:
         zed[c] = z_start(c, row[c])
+    for c in early:
+        gat[c] = ag_start(c, zed[c])
+    for c in late:
+        gat[c] = ag_start(c, zed[c])
     grads_end(1, copies_1)
-    for c in every:
-        gat[c] = ag_start(c, zed[c])
     grads_end(0, copies_0)
     for c in every:
         fw_start(c, *gat[c])
+    for copy in sides_0 + ends_0 + sides_1 + ends_1 + copies_0 + copies_1:
+        copy.wait_send()
+    for c in every:
+        for copy in [pair[c]] + row[c] + zed[c] + gat[c][0]:
+            copy.wait_send()
     for c in every:
         for copy in gat[c][1]:
-            copy.wait_recv()
+            copy.wait()
     full = total[...]
     scale = STEP_SIZE / jnp.sqrt(jnp.sum(full * full, keepdims=True) / full.size + EPSILON)
     for m in range(probe.shape[1]):
@@ -534,11 +546,6 @@
             new_ref[part, m] = (
                 probe[part, m] - scale * total[pl.ds((2 * m + part) * win, win)]
             )
-    for copy in halo_0 + halo_1 + copies_0 + copies_1:
-        copy.wait_send()
-    for c in every:
-        for copy in [pair[c]] + row[c] + zed[c] + gat[c][0] + gat[c][1]:
-            copy.wait_send()
 
 
 def out_kernel(grad, new, grad_out, new_out, sem):

time: 40.6 us -> 39 us (0.961)
  Pallas kernels: 39.6 us -> 38.2 us
    pallas_call x1, Pallas kernels: 38.4 us -> 37 us  [on_device(): pl.pallas_call(functools.partial(fused_kernel, (n_row, n_col, win, scans,...]
where the time goes in v3:
time: 39 us; the launch traced here: 38.8 us
  Pallas kernels  38.2 us (98%)
  between operations  0.64 us (2%)
    pallas_call x1, Pallas kernels, on_device(): pl.pallas_call(functools.partial(fused_kernel, (n_row, n_col, win, scans,...  37 us
    pallas_call x1, Pallas kernels, on_device(): pl.pallas_call(out_kernel, out_shape=(jax.ShapeDtypeStruct(object_tiles.s...  1.19 us

profile of v3, /device:TPU:0, one launch (start us, length us, event | category | flops | bytes accessed | tf_op | source)
XLA Modules:
  0.0 38.8 jit_solution(2058547140268168940)
XLA Ops:
  0.6 37.0 %shard_map.68 = (f32[2,2,256,256]{3,2,1,0:T(8,128)S(1)}, f32[2,4,128,128]{3,2,1,0:T(8,128)S(1)}) custom-call(s32[1,1,2,3]{3,2,1,0:T(2,128)} %bitcast.1, f32[2,2,256,256]{3,2,1,0:T(8,128)} %obj_hbm.1, f32[2,4,128,128]{3,2,1,0:T(8,128)} %probe_hbm.1, f32[1,1,3,128,128]{4,3,2,1,0:T(8,128)} %amp_hbm.1, bf16[8,256,256]{2,1,0:T(8,128)(2,1)} %constant.2.clone.tab_hbm), custom_call_target="tpu_custom_call" | custom-call | tf_op jit(solution)/shard_map/pallas_call | solution.py:582
  37.6 1.2 %shard_map.69 = (f32[2,2,256,256]{3,2,1,0:T(8,128)}, f32[2,4,128,128]{3,2,1,0:T(8,128)}) custom-call(f32[2,2,256,256]{3,2,1,0:T(8,128)S(1)} %get-tuple-element.4.grad, f32[2,4,128,128]{3,2,1,0:T(8,128)S(1)} %get-tuple-element.5.new), custom_call_target="tpu_custom_call" | custom-call | tf_op jit(solution)/shard_map/pallas_call | solution.py:645

commit v4 on v3

--- a/solution.py
+++ b/solution.py
@@ -133,11 +133,11 @@
     amp_hbm,
     tab_hbm,
     grad_ref,
-    new_ref,
+    total,
+    probe,
     off_ref,
     ext_0,
     ext_1,
-    probe,
     amp,
     tab,
     winds,
@@ -162,7 +162,6 @@
     half_sum,
     r_parts,
     z_parts,
-    total,
     in_sem,
     h_send,
     h_recv,
@@ -539,26 +538,26 @@
     for c in every:
         for copy in gat[c][1]:
             copy.wait()
-    full = total[...]
-    scale = STEP_SIZE / jnp.sqrt(jnp.sum(full * full, keepdims=True) / full.size + EPSILON)
-    for m in range(probe.shape[1]):
-        for part in range(2):
-            new_ref[part, m] = (
-                probe[part, m] - scale * total[pl.ds((2 * m + part) * win, win)]
-            )
-
-
-def out_kernel(grad, new, grad_out, new_out, sem):
-    copies = []
-    for part in range(2):
-        for lay in range(grad.shape[1]):
-            copies.append((grad.at[part, lay], grad_out.at[part, lay]))
-        copies.append((new.at[part], new_out.at[part]))
+
+
+def out_kernel(grad, total, probe, grad_out, new_out, new, sem):
+    count = grad.shape[1]
     copies = [
-        pltpu.make_async_copy(src, dst, sem.at[i]) for i, (src, dst) in enumerate(copies)
+        pltpu.make_async_copy(grad.at[i, j], grad_out.at[i, j], sem.at[i * count + j])
+        for i in range(2)
+        for j in range(count)
     ]
     for copy in copies:
         copy.start()
+    full = total[...]
+    win = probe.shape[2]
+    scale = STEP_SIZE / jnp.sqrt(jnp.sum(full * full, keepdims=True) / full.size + EPSILON)
+    for part in range(2):
+        for m in range(probe.shape[1]):
+            new[part, m] = probe[part, m] - scale * total[pl.ds((2 * m + part) * win, win)]
+        copy = pltpu.make_async_copy(new.at[part], new_out.at[part], sem.at[2 * count + part])
+        copy.start()
+        copies.append(copy)
     for copy in copies:
         copy.wait()
 
@@ -579,19 +578,19 @@
     block = lambda *shape: pltpu.VMEM(shape, F32)
     pairs = offsets.transpose(0, 1, 3, 2)
     table = jnp.asarray(tables(win))
-    grad, new = pl.pallas_call(
+    grad, total, probe = pl.pallas_call(
         functools.partial(fused_kernel, (n_row, n_col, win, scans, chunks)),
         out_shape=(
             jax.ShapeDtypeStruct(object_tiles.shape, F32),
+            jax.ShapeDtypeStruct((g_rows, win), F32),
             jax.ShapeDtypeStruct(probe_modes.shape, F32),
         ),
         in_specs=[hbm] * 5,
-        out_specs=(vmem, vmem),
+        out_specs=(vmem, vmem, vmem),
         scratch_shapes=[
             pltpu.SMEM(pairs.shape, jnp.int32),
             block(2, nt + 1, tall, LANES),
             block(2, nt + 1, tall, LANES),
-            block(*probe_modes.shape),
             block(*amplitude.shape),
             pltpu.VMEM(table.shape, BF16),
             block(scans, 4, win, win),
@@ -616,7 +615,6 @@
             block(g_rows // 2, win),
             block(n_row - 1, piece, win),
             block(n_z, piece, win),
-            block(g_rows, win),
             dma((4 * nt + 4,)),
             dma((2, 8)),
             dma((2, 8)),
@@ -648,11 +646,11 @@
             jax.ShapeDtypeStruct(object_tiles.shape, F32),
             jax.ShapeDtypeStruct(probe_modes.shape, F32),
         ),
-        in_specs=[vmem, vmem],
+        in_specs=[vmem, vmem, vmem],
         out_specs=(hbm, hbm),
-        scratch_shapes=[dma((6,))],
-        compiler_params=pltpu.CompilerParams(vmem_limit_bytes=1024 * 1024),
-    )(grad, new)
+        scratch_shapes=[block(*probe_modes.shape), dma((2 * object_tiles.shape[1] + 2,))],
+        compiler_params=pltpu.CompilerParams(vmem_limit_bytes=4 * 1024 * 1024),
+    )(grad, total, probe)
 
 
 CHUNKS = 2

time: 39 us -> 38.7 us (level)
  no operation moved by 1% of the time
where the time goes in v4:
time: 38.7 us; the launch traced here: 38.5 us
  Pallas kernels  37.9 us (98%)
  between operations  0.64 us (2%)
    pallas_call x1, Pallas kernels, on_device(): pl.pallas_call(functools.partial(fused_kernel, (n_row, n_col, win, scans,...  36.7 us
    pallas_call x1, Pallas kernels, on_device(): pl.pallas_call(out_kernel, out_shape=(jax.ShapeDtypeStruct(object_tiles.s...  1.19 us

profile of v4, /device:TPU:0, one launch (start us, length us, event | category | flops | bytes accessed | tf_op | source)
XLA Modules:
  0.0 38.5 jit_solution(17144510161119715814)
XLA Ops:
  0.6 36.7 %shard_map.68 = (f32[2,2,256,256]{3,2,1,0:T(8,128)S(1)}, f32[1024,128]{1,0:T(8,128)S(1)}, f32[2,4,128,128]{3,2,1,0:T(8,128)S(1)}) custom-call(s32[1,1,2,3]{3,2,1,0:T(2,128)} %bitcast.1, f32[2,2,256,256]{3,2,1,0:T(8,128)} %obj_hbm.1, f32[2,4,128,128]{3,2,1,0:T(8,128)} %probe_hbm.1, f32[1,1,3,128,128]{4,3,2,1,0:T(8,128)} %amp_hbm.1, ...), custom_call_target="tpu_custom_call" | custom-call | tf_op jit(solution)/shard_map/pallas_call | solution.py:581
  37.3 1.2 %shard_map.69 = (f32[2,2,256,256]{3,2,1,0:T(8,128)}, f32[2,4,128,128]{3,2,1,0:T(8,128)}) custom-call(f32[2,2,256,256]{3,2,1,0:T(8,128)S(1)} %get-tuple-element.5.grad, f32[1024,128]{1,0:T(8,128)S(1)} %get-tuple-element.6.total, f32[2,4,128,128]{3,2,1,0:T(8,128)S(1)} %get-tuple-element.7.probe), custom_call_target="tpu_custom_call" | custom-call | tf_op jit(solution)/shard_map/pallas_call | solution.py:643

commit v5 on v4

--- a/solution.py
+++ b/solution.py
@@ -194,7 +194,8 @@
     mates = {(dr % n_row, dc % n_col) for dr in (-1, 0, 1) for dc in (-1, 0, 1)}
     mates |= {(k, 0) for k in range(n_row)} | {(0, 2 * k) for k in range(n_z)}
     mates.discard((0, 0))
-    for mate in sorted(mates):
+    hops = lambda mate: min(mate[0], n_row - mate[0]) + min(mate[1], n_col - mate[1])
+    for mate in sorted(sorted(mates), key=hops, reverse=True):
         pl.semaphore_signal(barrier, inc=1, device_id=at(*mate), device_id_type=MESH)
     loads = []
     for lay in range(2):
@@ -210,7 +211,7 @@
     per_lay = len(loads) // 2
     for src, dst in ((off_hbm, off_ref), (probe_hbm, probe), (tab_hbm, tab), (amp_hbm, amp)):
         loads.append(pltpu.make_async_copy(src, dst, in_sem.at[len(loads)]))
-    for load in loads:
+    for load in loads[: 2 * per_lay + 1]:
         load.start()
 
     head, tail = pl.ds(0, FOLD), pl.ds((tile - HALO) // 2, FOLD)
@@ -280,6 +281,8 @@
     sides_1 = halo_start(1, sides)
     ends_0 = halo_start(0, ends)
     ends_1 = halo_start(1, ends)
+    for load in loads[2 * per_lay + 1 :]:
+        load.start()
     gprobe[...] = jnp.zeros_like(gprobe)
     gobj[...] = jnp.zeros_like(gobj)
     zpad[...] = jnp.zeros_like(zpad)

time: 38.7 us -> 38.7 us (level)
  no operation moved by 1% of the time
where the time goes in v5:
time: 38.7 us; the launch traced here: 38.6 us
  Pallas kernels  37.9 us (98%)
  between operations  0.64 us (2%)
    pallas_call x1, Pallas kernels, on_device(): pl.pallas_call(functools.partial(fused_kernel, (n_row, n_col, win, scans,...  36.7 us
    pallas_call x1, Pallas kernels, on_device(): pl.pallas_call(out_kernel, out_shape=(jax.ShapeDtypeStruct(object_tiles.s...  1.19 us

profile of v5, /device:TPU:0, one launch (start us, length us, event | category | flops | bytes accessed | tf_op | source)
XLA Modules:
  0.0 38.6 jit_solution(15186258518626995881)
XLA Ops:
  0.6 36.7 %shard_map.68 = (f32[2,2,256,256]{3,2,1,0:T(8,128)S(1)}, f32[1024,128]{1,0:T(8,128)S(1)}, f32[2,4,128,128]{3,2,1,0:T(8,128)S(1)}) custom-call(s32[1,1,2,3]{3,2,1,0:T(2,128)} %bitcast.1, f32[2,2,256,256]{3,2,1,0:T(8,128)} %obj_hbm.1, f32[2,4,128,128]{3,2,1,0:T(8,128)} %probe_hbm.1, f32[1,1,3,128,128]{4,3,2,1,0:T(8,128)} %amp_hbm.1, ...), custom_call_target="tpu_custom_call" | custom-call | tf_op jit(solution)/shard_map/pallas_call | solution.py:584
  37.4 1.2 %shard_map.69 = (f32[2,2,256,256]{3,2,1,0:T(8,128)}, f32[2,4,128,128]{3,2,1,0:T(8,128)}) custom-call(f32[2,2,256,256]{3,2,1,0:T(8,128)S(1)} %get-tuple-element.5.grad, f32[1024,128]{1,0:T(8,128)S(1)} %get-tuple-element.6.total, f32[2,4,128,128]{3,2,1,0:T(8,128)S(1)} %get-tuple-element.7.probe), custom_call_target="tpu_custom_call" | custom-call | tf_op jit(solution)/shard_map/pallas_call | solution.py:646

commit v6 on v5

--- a/solution.py
+++ b/solution.py
@@ -358,12 +358,15 @@
             for part in range(2):
                 block = pltpu.roll(gobj[lay, part, s], rem, 1)
                 for t in range(nt + 1):
-                    zpad[s, part, t, pl.ds(pad, win), :] = jnp.where(where == t, block, 0.0)
+                    zpad[lay, s, part, t, pl.ds(pad, win), :] = jnp.where(where == t, block, 0.0)
+        return starts
+
+    def gather(lay, starts, tiles):
         for part in range(2):
-            for t in range(nt + 1):
+            for t in tiles:
                 value = None
                 for s in range(scans):
-                    block = zpad[s, part, t, pl.ds(starts[s], tall), :]
+                    block = zpad[lay, s, part, t, pl.ds(starts[s], tall), :]
                     value = block if value is None else value + block
                 acc[lay, part, t] = value
 
@@ -505,7 +508,8 @@
         pair[c] = pair_start(c)
     for s in range(scans):
         first_half(1, s)
-    place(1)
+    starts = place(1)
+    gather(1, starts, (nt,))
     grads_fold(1)
     copies_1 = grads_start(1, (4, 5, 6, 7, 2, 3))
     for c in early:
@@ -514,7 +518,9 @@
         second_half(1, s)
     for c in late:
         pair[c] = pair_start(c)
-    place(0)
+    gather(1, starts, range(nt))
+    starts = place(0)
+    gather(0, starts, range(nt + 1))
     grads_fold(0)
     copies_0 = grads_start(0, (4, 5, 6, 7, 2, 3))
     for c in late:
@@ -602,7 +608,7 @@
             block(scans, win, win),
             block(2, 2, scans, win, win),
             block(g_rows, win),
-            block(scans, 2, nt + 1, 2 * tall - win, LANES),
+            block(2, scans, 2, nt + 1, 2 * tall - win, LANES),
             block(2, 2, nt + 1, tall, LANES),
             block(2, tile // 2, LANES),
             block(2, tile // 2, LANES),

time: 38.7 us -> 38.7 us (level)
  no operation moved by 1% of the time
where the time goes in v6:
time: 38.7 us; the launch traced here: 38.5 us
  Pallas kernels  37.9 us (98%)
  between operations  0.64 us (2%)
    pallas_call x1, Pallas kernels, on_device(): pl.pallas_call(functools.partial(fused_kernel, (n_row, n_col, win, scans,...  36.7 us
    pallas_call x1, Pallas kernels, on_device(): pl.pallas_call(out_kernel, out_shape=(jax.ShapeDtypeStruct(object_tiles.s...  1.19 us

profile of v6, /device:TPU:0, one launch (start us, length us, event | category | flops | bytes accessed | tf_op | source)
XLA Modules:
  0.0 38.5 jit_solution(2284381186219137840)
XLA Ops:
  0.6 36.7 %shard_map.68 = (f32[2,2,256,256]{3,2,1,0:T(8,128)S(1)}, f32[1024,128]{1,0:T(8,128)S(1)}, f32[2,4,128,128]{3,2,1,0:T(8,128)S(1)}) custom-call(s32[1,1,2,3]{3,2,1,0:T(2,128)} %bitcast.1, f32[2,2,256,256]{3,2,1,0:T(8,128)} %obj_hbm.1, f32[2,4,128,128]{3,2,1,0:T(8,128)} %probe_hbm.1, f32[1,1,3,128,128]{4,3,2,1,0:T(8,128)} %amp_hbm.1, ...), custom_call_target="tpu_custom_call" | custom-call | tf_op jit(solution)/shard_map/pallas_call | solution.py:590
  37.4 1.2 %shard_map.69 = (f32[2,2,256,256]{3,2,1,0:T(8,128)}, f32[2,4,128,128]{3,2,1,0:T(8,128)}) custom-call(f32[2,2,256,256]{3,2,1,0:T(8,128)S(1)} %get-tuple-element.5.grad, f32[1024,128]{1,0:T(8,128)S(1)} %get-tuple-element.6.total, f32[2,4,128,128]{3,2,1,0:T(8,128)S(1)} %get-tuple-element.7.probe), custom_call_target="tpu_custom_call" | custom-call | tf_op jit(solution)/shard_map/pallas_call | solution.py:652
